TPU v7x, 512 devices: a whole 4x8x8 slice. The times are simulated.
512 devices in a mesh: mp: 16 (over x_lo, y), dp: 32 (over x_hi, z, core).
Axes of the slice: x: 4 (x_hi: 2, x_lo: 2; x = x_hi * 2 + x_lo), y: 8, z: 8, core: 2. Of those that a mesh axis runs over, the one named last changes fastest.
Arguments:
- activations: bfloat16 [16, 2048, 8192], P('mp', 'dp'), may hold values from -54 to 54
- cotangents: bfloat16 [16, 2048, 1792], P('mp', 'dp'), may hold values from -54 to 54
- label_mask: int32 [16, 2048], P('mp', 'dp'), may hold values from 0 to 1, as said below
- checkpoints: bfloat16 [16, 8192, 1792], P('mp', 'dp'), may hold values from -6 to 6
Outputs:
- merged: bfloat16 [8192, 1792], P('dp')
Inputs may be any that keep to these rules, and one draw needn't show every extreme that they name: `label_mask`: the last token of every checkpoint is labelled.
All inputs are finite; a program needn't handle non-finite values.
Results may differ from a plain program's by a relative error of at most 0.0025.
Values may be sent and summed in bfloat16 or wider, within the bound.
A program may use at most 64 MiB of HBM per device.

v0:
```python
import jax
import jax.numpy as jnp
from jax import lax
from jax.sharding import PartitionSpec as P


def contract_tokens(feature_sq, block_cot):
    return lax.dot_general(
        feature_sq, block_cot, (((0,), (0,)), ((), ())), preferred_element_type=jnp.float32
    )


def per_device(activations, cotangents, label_mask, checkpoints):
    tok_acts = activations[0]
    tok_mask = label_mask[0]
    own_slab = checkpoints[0]
    label_weight = tok_mask.astype(jnp.float32)
    cot_square = (label_weight[:, None] * jnp.square(cotangents[0].astype(jnp.float32))).astype(
        jnp.bfloat16
    )
    act_square = jnp.square(tok_acts.astype(jnp.float32)).astype(jnp.bfloat16)
    feature_sq = lax.all_to_all(act_square, "dp", split_axis=1, concat_axis=0, tiled=True)
    fisher_sum = contract_tokens(feature_sq, lax.all_gather(cot_square, "dp", axis=0, tiled=True))
    labelled = lax.psum(jnp.sum(label_weight), "dp")
    fisher = fisher_sum / labelled
    weighted = fisher * own_slab.astype(jnp.float32)
    numerator, denominator = lax.psum((weighted, fisher), "mp")
    merged = (numerator / denominator).astype(jnp.bfloat16)
    return merged


def solution(mesh):
    return jax.shard_map(
        per_device,
        mesh=mesh,
        in_specs=(P("mp", "dp", None), P("mp", "dp", None), P("mp", "dp"), P("mp", "dp", None)),
        out_specs=P("dp", None),
        check_vma=False,
    )
```

profile of v0, /device:TPU:4, one launch (start us, length us, event | category | flops | bytes accessed | tf_op | source)
XLA Modules:
  0.0 296.8 jit_solution(10089826524948816606)
XLA Ops:
  6.5 0.0 all-gather.2.cloned.1.call-start
  6.5 0.7 convert_bitcast_fusion
  7.2 1.7 fusion
  8.9 0.0 all-gather.2.cloned.1.call-update
  8.9 1.4 multiply_convert_fusion
  10.3 0.3 copy.7
  10.6 0.0 copy-start.1
  10.6 0.0 copy-start
  10.6 1.6 copy.6
  12.2 13.4 %all-to-all-start = ((bf16[64,32,256]{2,0,1:T(8,128)(2,1)}), bf16[64,32,256]{2,0,1:T(8,128)(2,1)S(1)}, u32[]{:S(2)}, u32[]{:S(2)}) async-start(bf16[64,32,256]{2,0,1:T(8,128)(2,1)} %copy.6), calls=%async_computation | async-start | bytes 2097152 | tf_op jit(solution)/shard_map/all_to_all | solution.py:22
  25.7 0.0 all-reduce.3.cloned.1.call-start
  25.7 0.0 copy-done.1
  25.7 0.6 convert_reduce_fusion
  26.3 88.2 %psum.21 = f32[]{:T(128)} all-reduce(f32[]{:T(128)} %convert_reduce_fusion), channel_id=1, replica_groups=mesh['mp'=16,'dp'=32] {'dp'}, use_global_device_ids=true, to_apply=%region_1.0 | all-reduce | flops 1 | bytes 8 | tf_op jit(solution)/shard_map/psum | solution.py:24
  114.5 0.0 all-to-all-done
  114.5 9.9 %all-gather.2.cloned.1.call-done = bf16[2048,1792]{1,0:T(8,128)(2,1)} async-done(((bf16[64,1792]{1,0:T(8,128)(2,1)}), bf16[2048,1792]{1,0:T(8,128)(2,1)}) %all-gather.2.cloned.1.call-update) | async-done | bytes 7340048 | tf_op jit(solution)/shard_map/all_gather | solution.py:23
  124.4 0.0 copy-done
  124.4 7.7 %convert_multiply_fusion = (f32[256,1792]{1,0:T(8,128)}, f32[256,1792]{1,0:T(8,128)}) fusion(bf16[1,256,1792]{2,1,0:T(8,128)(2,1)S(1)} %copy-done, f32[]{:T(128)} %psum.21, bf16[2048,256]{1,0:T(8,128)(2,1)S(1)} %bitcast.19, bf16[2048,1792]{1,0:T(8,128)(2,1)} %all-gather.2.cloned.1.call-done), kind=kOutput, calls=%fused_computation.2 | convolution fusion | flops 1880424448 | bytes 12976132 | tf_op jit(solution)/shard_map/dot_general | solution.py:8
  132.1 0.0 all-reduce.3.cloned.1.call-update
  132.1 154.6 %all-reduce.3.cloned.1.call-done = (f32[256,1792]{1,0:T(8,128)}, f32[256,1792]{1,0:T(8,128)}) async-done(((f32[256,1792]{1,0:T(8,128)}, f32[256,1792]{1,0:T(8,128)}), (f32[256,1792]{1,0:T(8,128)}, f32[256,1792]{1,0:T(8,128)})) %all-reduce.3.cloned.1.call-update) | async-done | bytes 3670032 | tf_op jit(solution)/shard_map/psum | solution.py:27
  286.7 3.2 %divide_convert_fusion = bf16[256,1792]{1,0:T(8,128)(2,1)} fusion(f32[256,1792]{1,0:T(8,128)} %get-tuple-element.5, f32[256,1792]{1,0:T(8,128)} %get-tuple-element.6), kind=kLoop, calls=%fused_computation.3 | loop fusion | flops 917504 | bytes 4587520 | tf_op jit(solution)/shard_map/convert_element_type | solution.py:28
Async XLA Ops:
  6.5 117.9 %all-gather.2.cloned.1.call-start = ((), (), s32[]{:S(2)}) async-start(), calls=%async_computation.1 | async-start | bytes 7569408 | tf_op jit(solution)/shard_map/all_gather | solution.py:23
  10.6 15.1 %copy-start.1 = (s32[1,64]{1,0:T(1,128)S(1)}, s32[1,64]{1,0:T(1,128)}, u32[]{:S(2)}) copy-start(s32[1,64]{1,0:T(1,128)} %param.6) | copy-start | bytes 772
  10.6 113.8 %copy-start = (bf16[1,256,1792]{2,1,0:T(8,128)(2,1)S(1)}, bf16[1,256,1792]{2,1,0:T(8,128)(2,1)}, u32[]{:S(2)}) copy-start(bf16[1,256,1792]{2,1,0:T(8,128)(2,1)} %param.7) | copy-start | bytes 2752516
  12.2 102.3 %all-to-all-start = ((bf16[64,32,256]{2,0,1:T(8,128)(2,1)}), bf16[64,32,256]{2,0,1:T(8,128)(2,1)S(1)}, u32[]{:S(2)}, u32[]{:S(2)}) async-start(bf16[64,32,256]{2,0,1:T(8,128)(2,1)} %copy.6), calls=%async_computation | async-start | bytes 2097152 | tf_op jit(solution)/shard_map/all_to_all | solution.py:22
  25.7 261.1 %all-reduce.3.cloned.1.call-start = ((), (), s32[]{:S(2)}) async-start(), calls=%async_computation.2 | async-start | bytes 7340032 | tf_op jit(solution)/shard_map/psum | solution.py:27
Sparse Core Ops, SparseCore 0:
  10.7 113.6 all-gather.1
  132.3 154.4 all-reduce.2
where the time goes:
time: 297 us
  waiting for transfers between devices  165 us (56%)
  blocking collectives  88.2 us (30%)
  starting transfers between devices  13.5 us (5%)
  between operations  13.4 us (5%)
  matrix products  7.7 us (3%)
  other arithmetic  7.61 us (3%)
    psum x1, waiting for transfers between devices, per_device(): numerator, denominator = lax.psum((weighted, fisher), 'mp')  155 us
    psum x1, blocking collectives, per_device(): labelled = lax.psum(jnp.sum(label_weight), 'dp')  88.2 us
    all_to_all x1, starting transfers between devices, per_device(): lax.all_to_all(act_square, 'dp', split_axis=1, concat_axis=0, tiled=True)  13.4 us
    all_gather x1, waiting for transfers between devices, per_device(): lax.all_gather(cot_square, 'dp', axis=0, tiled=True)  9.88 us
    dot_general x1, matrix products, contract_tokens(): lax.dot_general(feature_sq, block_cot, (((0,), (0,)), ((), ())), preferre...  7.7 us
  transfers between devices with their start and end apart: 3, of which 2 were waited for; matrix products, arithmetic and copies ran while one was open for 1% of the time, Pallas kernels for 0%

commit v1 on v0

--- a/solution.py
+++ b/solution.py
@@ -20,7 +20,12 @@
     )
     act_square = jnp.square(tok_acts.astype(jnp.float32)).astype(jnp.bfloat16)
     feature_sq = lax.all_to_all(act_square, "dp", split_axis=1, concat_axis=0, tiled=True)
-    fisher_sum = contract_tokens(feature_sq, lax.all_gather(cot_square, "dp", axis=0, tiled=True))
+    fisher_sum = contract_tokens(
+        feature_sq,
+        jnp.concatenate(
+            lax.all_to_all(jnp.stack([cot_square] * lax.axis_size("dp")), "dp", 0, 0), axis=0
+        ),
+    )
     labelled = lax.psum(jnp.sum(label_weight), "dp")
     fisher = fisher_sum / labelled
     weighted = fisher * own_slab.astype(jnp.float32)

time: 297 us -> 450 us (1.52)
  blocking collectives: 88.2 us -> 217 us
  waiting for transfers between devices: 165 us -> 180 us
  starting transfers between devices: 13.5 us -> 21.1 us
    psum x1, blocking collectives: 88.2 us -> 217 us  [per_device(): labelled = lax.psum(jnp.sum(label_weight), 'dp')]
    all_to_all x1, waiting for transfers between devices: 0.01 us -> 27.1 us  [per_device(): lax.all_to_all(act_square, 'dp', split_axis=1, concat_axis=0, tiled=True)]
    all_gather x1 -> x0, waiting for transfers between devices: 9.88 us -> none  [per_device(): lax.all_gather(cot_square, 'dp', axis=0, tiled=True)]
    all_to_all x0 -> x1, starting transfers between devices: none -> 7.57 us  [per_device(): lax.all_to_all(jnp.stack([cot_square] * lax.axis_size('dp')), 'dp', 0, 0)]
  transfers between devices with their start and end apart: 3 -> 3, of which waited for: 2 -> 2; matrix products, arithmetic and copies ran while one was open for 1% -> 0% of each run, Pallas kernels for 0% -> 0%
where the time goes in v1:
time: 450 us
  blocking collectives  217 us (48%)
  waiting for transfers between devices  180 us (40%)
  starting transfers between devices  21.1 us (5%)
  between operations  13.5 us (3%)
  matrix products  7.72 us (2%)
  local copies, waits for them, and re-layouts  5.68 us (1%)
  other arithmetic  5.31 us (1%)
    psum x1, blocking collectives, per_device(): labelled = lax.psum(jnp.sum(label_weight), 'dp')  217 us
    psum x1, waiting for transfers between devices, per_device(): numerator, denominator = lax.psum((weighted, fisher), 'mp')  153 us
    all_to_all x1, waiting for transfers between devices, per_device(): lax.all_to_all(act_square, 'dp', split_axis=1, concat_axis=0, tiled=True)  27.1 us
    all_to_all x1, starting transfers between devices, per_device(): lax.all_to_all(act_square, 'dp', split_axis=1, concat_axis=0, tiled=True)  13.4 us
  transfers between devices with their start and end apart: 3, of which 2 were waited for; matrix products, arithmetic and copies ran while one was open for 0% of the time, Pallas kernels for 0%

profile of v1, /device:TPU:4, one launch (start us, length us, event | category | flops | bytes accessed | tf_op | source)
XLA Modules:
  0.0 449.7 jit_solution(17766040786689214350)
XLA Ops:
  6.5 1.4 multiply_convert_fusion
  7.9 0.3 copy.6
  8.2 0.0 copy-start.2
  8.2 0.0 copy-start
  8.2 1.5 copy.5
  9.8 13.4 %all-to-all-start = ((bf16[64,32,256]{2,0,1:T(8,128)(2,1)}), bf16[64,32,256]{2,0,1:T(8,128)(2,1)S(1)}, u32[]{:S(2)}, u32[]{:S(2)}) async-start(bf16[64,32,256]{2,0,1:T(8,128)(2,1)} %copy.5), calls=%async_computation | async-start | bytes 2097152 | tf_op jit(solution)/shard_map/all_to_all | solution.py:22
  23.2 0.0 copy-done.2
  23.2 0.0 copy-done
  23.3 0.1 fusion.2
  23.4 27.1 %all-to-all-done = bf16[64,32,256]{2,0,1:T(8,128)(2,1)S(1)} async-done(((bf16[64,32,256]{2,0,1:T(8,128)(2,1)}), bf16[64,32,256]{2,0,1:T(8,128)(2,1)S(1)}, u32[]{:S(2)}, u32[]{:S(2)}) %all-to-all-start) | async-done | bytes 1048608 | tf_op jit(solution)/shard_map/all_to_all | solution.py:22
  50.5 3.9 stack.5
  54.4 0.0 copy-start.1
  54.4 7.6 %all-to-all-start.1 = ((bf16[32,64,1792]{2,1,0:T(8,128)(2,1)}), bf16[32,64,1792]{2,1,0:T(8,128)(2,1)}, u32[]{:S(2)}, u32[]{:S(2)}) async-start(bf16[32,64,1792]{2,1,0:T(8,128)(2,1)} %stack.5), calls=%async_computation.1 | async-start | bytes 14680064 | tf_op jit(solution)/shard_map/all_to_all | solution.py:26
  61.9 0.0 all-reduce.3.cloned.1.call-start
  62.0 0.6 convert_reduce_fusion
  62.6 216.6 %psum.21 = f32[]{:T(128)} all-reduce(f32[]{:T(128)} %convert_reduce_fusion), channel_id=1, replica_groups=mesh['mp'=16,'dp'=32] {'dp'}, use_global_device_ids=true, to_apply=%region_1.0 | all-reduce | flops 1 | bytes 8 | tf_op jit(solution)/shard_map/psum | solution.py:29
  279.1 0.0 all-to-all-done.1
  279.1 0.0 copy-done.1
  279.1 7.7 %convert_multiply_fusion = (f32[256,1792]{1,0:T(8,128)}, f32[256,1792]{1,0:T(8,128)}) fusion(bf16[1,256,1792]{2,1,0:T(8,128)(2,1)S(1)} %copy-done.1, f32[]{:T(128)} %psum.21, bf16[32,64,1792]{2,1,0:T(8,128)(2,1)} %all-to-all-done.1, bf16[64,32,256]{2,0,1:T(8,128)(2,1)S(1)} %all-to-all-done), kind=kOutput, calls=%fused_computation.3 | convolution fusion | flops 1880424448 | bytes 12976132 | tf_op jit(solution)/shard_map/dot_general | solution.py:8
  286.9 0.0 all-reduce.3.cloned.1.call-update
  286.9 152.8 %all-reduce.3.cloned.1.call-done = (f32[256,1792]{1,0:T(8,128)}, f32[256,1792]{1,0:T(8,128)}) async-done(((f32[256,1792]{1,0:T(8,128)}, f32[256,1792]{1,0:T(8,128)}), (f32[256,1792]{1,0:T(8,128)}, f32[256,1792]{1,0:T(8,128)})) %all-reduce.3.cloned.1.call-update) | async-done | bytes 3670032 | tf_op jit(solution)/shard_map/psum | solution.py:32
  439.6 3.2 divide_convert_fusion
  (1 shorter events, 0.0 us)
Async XLA Ops:
  8.2 15.0 %copy-start.2 = (s32[1,64]{1,0:T(1,128)S(1)}, s32[1,64]{1,0:T(1,128)}, u32[]{:S(2)}) copy-start(s32[1,64]{1,0:T(1,128)} %param.6) | copy-start | bytes 772
  8.2 15.0 %copy-start = (bf16[1,64,1792]{2,1,0:T(8,128)(2,1)S(1)}, bf16[1,64,1792]{2,1,0:T(8,128)(2,1)}, u32[]{:S(2)}) copy-start(bf16[1,64,1792]{2,1,0:T(8,128)(2,1)} %param.5) | copy-start | bytes 688132
  9.8 40.7 %all-to-all-start = ((bf16[64,32,256]{2,0,1:T(8,128)(2,1)}), bf16[64,32,256]{2,0,1:T(8,128)(2,1)S(1)}, u32[]{:S(2)}, u32[]{:S(2)}) async-start(bf16[64,32,256]{2,0,1:T(8,128)(2,1)} %copy.5), calls=%async_computation | async-start | bytes 2097152 | tf_op jit(solution)/shard_map/all_to_all | solution.py:22
  54.4 224.8 %copy-start.1 = (bf16[1,256,1792]{2,1,0:T(8,128)(2,1)S(1)}, bf16[1,256,1792]{2,1,0:T(8,128)(2,1)}, u32[]{:S(2)}) copy-start(bf16[1,256,1792]{2,1,0:T(8,128)(2,1)} %param.7) | copy-start | bytes 2752516
  54.4 224.8 %all-to-all-start.1 = ((bf16[32,64,1792]{2,1,0:T(8,128)(2,1)}), bf16[32,64,1792]{2,1,0:T(8,128)(2,1)}, u32[]{:S(2)}, u32[]{:S(2)}) async-start(bf16[32,64,1792]{2,1,0:T(8,128)(2,1)} %stack.5), calls=%async_computation.1 | async-start | bytes 14680064 | tf_op jit(solution)/shard_map/all_to_all | solution.py:26
  61.9 377.7 %all-reduce.3.cloned.1.call-start = ((), (), s32[]{:S(2)}) async-start(), calls=%async_computation.2 | async-start | bytes 7340032 | tf_op jit(solution)/shard_map/psum | solution.py:32
Sparse Core Ops, SparseCore 0:
  287.0 152.5 all-reduce.2

commit v2 on v0

--- a/solution.py
+++ b/solution.py
@@ -19,7 +19,10 @@
         jnp.bfloat16
     )
     act_square = jnp.square(tok_acts.astype(jnp.float32)).astype(jnp.bfloat16)
-    feature_sq = lax.all_to_all(act_square, "dp", split_axis=1, concat_axis=0, tiled=True)
+    feature_sq = jnp.concatenate(
+        lax.all_to_all(jnp.stack(jnp.split(act_square, lax.axis_size("dp"), axis=1)), "dp", 0, 0),
+        axis=0,
+    )
     fisher_sum = contract_tokens(feature_sq, lax.all_gather(cot_square, "dp", axis=0, tiled=True))
     labelled = lax.psum(jnp.sum(label_weight), "dp")
     fisher = fisher_sum / labelled

time: 297 us -> 304 us (1.024)
  local copies, waits for them, and re-layouts: 1.85 us -> 19.7 us
  waiting for transfers between devices: 165 us -> 154 us
    unnamed x5 -> x35, local copies, waits for them, and re-layouts: 0.27 us -> 19.1 us
    all_gather x1, waiting for transfers between devices: 9.88 us -> 0.01 us  [per_device(): lax.all_gather(cot_square, 'dp', axis=0, tiled=True)]
  transfers between devices with their start and end apart: 3 -> 3, of which waited for: 2 -> 1; matrix products, arithmetic and copies ran while one was open for 1% -> 7% of each run, Pallas kernels for 0% -> 0%
where the time goes in v2:
time: 304 us; the launch traced here: 303 us
  waiting for transfers between devices  154 us (51%)
  blocking collectives  87.4 us (29%)
  local copies, waits for them, and re-layouts  19.7 us (6%)
  starting transfers between devices  13.5 us (4%)
  between operations  13.4 us (4%)
  matrix products  7.71 us (3%)
  other arithmetic  7.61 us (3%)
    psum x1, waiting for transfers between devices, per_device(): numerator, denominator = lax.psum((weighted, fisher), 'mp')  154 us
    psum x1, blocking collectives, per_device(): labelled = lax.psum(jnp.sum(label_weight), 'dp')  87.4 us
    unnamed x35, local copies, waits for them, and re-layouts  19.1 us
    all_to_all x1, starting transfers between devices, per_device(): lax.all_to_all(jnp.stack(jnp.split(act_square, lax.axis_size('dp'), axis=...  13.4 us
    dot_general x1, matrix products, contract_tokens(): lax.dot_general(feature_sq, block_cot, (((0,), (0,)), ((), ())), preferre...  7.71 us
  transfers between devices with their start and end apart: 3, of which 1 were waited for; matrix products, arithmetic and copies ran while one was open for 7% of the time, Pallas kernels for 0%

profile of v2, /device:TPU:4, one launch (start us, length us, event | category | flops | bytes accessed | tf_op | source)
XLA Modules:
  0.0 303.5 jit_solution(4291136958018169059)
XLA Ops:
  6.5 0.0 all-gather.2.cloned.1.call-start
  6.5 0.7 convert_bitcast_fusion
  7.2 1.7 fusion.1
  8.9 0.0 all-gather.2.cloned.1.call-update
  8.9 1.4 fusion
  10.3 0.6 constant_dynamic-update-slice_fusion.31
  11.0 0.6 constant_dynamic-update-slice_fusion.30
  11.6 0.6 constant_dynamic-update-slice_fusion.29
  12.2 0.6 constant_dynamic-update-slice_fusion.28
  12.8 0.6 constant_dynamic-update-slice_fusion.27
  13.4 0.6 constant_dynamic-update-slice_fusion.26
  14.0 0.6 constant_dynamic-update-slice_fusion.25
  14.7 0.6 constant_dynamic-update-slice_fusion.24
  15.3 0.6 constant_dynamic-update-slice_fusion.23
  15.9 0.6 constant_dynamic-update-slice_fusion.22
  16.5 0.6 constant_dynamic-update-slice_fusion.21
  17.1 0.6 constant_dynamic-update-slice_fusion.20
  17.7 0.6 constant_dynamic-update-slice_fusion.19
  18.4 0.6 constant_dynamic-update-slice_fusion.18
  19.0 0.6 constant_dynamic-update-slice_fusion.17
  19.6 0.6 constant_dynamic-update-slice_fusion.16
  20.2 0.6 constant_dynamic-update-slice_fusion.15
  20.8 0.6 constant_dynamic-update-slice_fusion.14
  21.4 0.6 constant_dynamic-update-slice_fusion.13
  22.0 0.6 constant_dynamic-update-slice_fusion.12
  22.7 0.6 constant_dynamic-update-slice_fusion.11
  23.3 0.6 constant_dynamic-update-slice_fusion.10
  23.9 0.6 constant_dynamic-update-slice_fusion.9
  24.5 0.6 constant_dynamic-update-slice_fusion.8
  25.1 0.6 constant_dynamic-update-slice_fusion.7
  25.7 0.6 constant_dynamic-update-slice_fusion.6
  26.4 0.6 constant_dynamic-update-slice_fusion.5
  27.0 0.6 constant_dynamic-update-slice_fusion.4
  27.6 0.6 constant_dynamic-update-slice_fusion.3
  28.2 0.6 constant_dynamic-update-slice_fusion.2
  28.8 0.6 constant_dynamic-update-slice_fusion.1
  29.5 0.6 constant_dynamic-update-slice_fusion
  30.1 13.4 %all-to-all-start = ((bf16[32,64,256]{2,1,0:T(8,128)(2,1)}), bf16[32,64,256]{2,1,0:T(8,128)(2,1)S(1)}, u32[]{:S(2)}, u32[]{:S(2)}) async-start(bf16[32,64,256]{2,1,0:T(8,128)(2,1)} %constant_dynamic-update-slice_fusion), calls=%async_computation | async-start | bytes 2097152 | tf_op jit(solution)/shard_map/all_to_all | solution.py:23
  43.5 0.0 all-reduce.3.cloned.1.call-start
  43.6 0.0 copy-done.1
  43.6 0.6 convert_reduce_fusion
  44.2 87.4 %psum.21 = f32[]{:T(128)} all-reduce(f32[]{:T(128)} %convert_reduce_fusion), channel_id=1, replica_groups=mesh['mp'=16,'dp'=32] {'dp'}, use_global_device_ids=true, to_apply=%region_1.0 | all-reduce | flops 1 | bytes 8 | tf_op jit(solution)/shard_map/psum | solution.py:27
  131.6 0.0 all-to-all-done
  131.6 0.0 copy-done
  131.6 7.7 %convert_multiply_fusion = (f32[256,1792]{1,0:T(8,128)}, f32[256,1792]{1,0:T(8,128)}) fusion(bf16[1,256,1792]{2,1,0:T(8,128)(2,1)S(1)} %copy-done, f32[]{:T(128)} %psum.21, bf16[2048,256]{1,0:T(8,128)(2,1)S(1)} %bitcast.142, bf16[2048,1792]{1,0:T(8,128)(2,1)} %all-gather.2.cloned.1.call-done), kind=kOutput, calls=%fused_computation.2 | convolution fusion | flops 1880424448 | bytes 12976132 | tf_op jit(solution)/shard_map/dot_general | solution.py:8
  139.3 0.0 all-reduce.3.cloned.1.call-update
  139.4 154.0 %all-reduce.3.cloned.1.call-done = (f32[256,1792]{1,0:T(8,128)}, f32[256,1792]{1,0:T(8,128)}) async-done(((f32[256,1792]{1,0:T(8,128)}, f32[256,1792]{1,0:T(8,128)}), (f32[256,1792]{1,0:T(8,128)}, f32[256,1792]{1,0:T(8,128)})) %all-reduce.3.cloned.1.call-update) | async-done | bytes 3670032 | tf_op jit(solution)/shard_map/psum | solution.py:30
  293.4 3.2 %divide_convert_fusion = bf16[256,1792]{1,0:T(8,128)(2,1)} fusion(f32[256,1792]{1,0:T(8,128)} %get-tuple-element.5, f32[256,1792]{1,0:T(8,128)} %get-tuple-element.6), kind=kLoop, calls=%fused_computation.3 | loop fusion | flops 917504 | bytes 4587520 | tf_op jit(solution)/shard_map/convert_element_type | solution.py:31
  (3 shorter events, 0.0 us)
Async XLA Ops:
  6.5 125.1 %all-gather.2.cloned.1.call-start = ((), (), s32[]{:S(2)}) async-start(), calls=%async_computation.1 | async-start | bytes 7569408 | tf_op jit(solution)/shard_map/all_gather | solution.py:26
  15.3 28.3 %copy-start.1 = (s32[1,64]{1,0:T(1,128)S(1)}, s32[1,64]{1,0:T(1,128)}, u32[]{:S(2)}) copy-start(s32[1,64]{1,0:T(1,128)} %param.6) | copy-start | bytes 772
  15.3 116.4 %copy-start = (bf16[1,256,1792]{2,1,0:T(8,128)(2,1)S(1)}, bf16[1,256,1792]{2,1,0:T(8,128)(2,1)}, u32[]{:S(2)}) copy-start(bf16[1,256,1792]{2,1,0:T(8,128)(2,1)} %param.7) | copy-start | bytes 2752516
  30.1 101.6 %all-to-all-start = ((bf16[32,64,256]{2,1,0:T(8,128)(2,1)}), bf16[32,64,256]{2,1,0:T(8,128)(2,1)S(1)}, u32[]{:S(2)}, u32[]{:S(2)}) async-start(bf16[32,64,256]{2,1,0:T(8,128)(2,1)} %constant_dynamic-update-slice_fusion), calls=%async_computation | async-start | bytes 2097152 | tf_op jit(solution)/shard_map/all_to_all | solution.py:23
  43.5 249.9 %all-reduce.3.cloned.1.call-start = ((), (), s32[]{:S(2)}) async-start(), calls=%async_computation.2 | async-start | bytes 7340032 | tf_op jit(solution)/shard_map/psum | solution.py:30
Sparse Core Ops, SparseCore 0:
  10.7 112.3 all-gather.1
  139.5 153.8 all-reduce.2
